TPU v7x, 256 devices: a whole 4x4x8 slice. The times are simulated.
256 devices in a mesh: req: 16 (over y, x_hi, core), tp: 16 (over x_lo, z).
Axes of the slice: x: 4 (x_hi: 2, x_lo: 2; x = x_hi * 2 + x_lo), y: 4, z: 8, core: 2. Of those that a mesh axis runs over, the one named last changes fastest.
Arguments:
- patches: bfloat16 [16, 1024, 1664], P('req', 'tp'), may hold values from -6 to 6
- vis_gain: float32 [1664], replicated, may hold values from 0.1 to 1.9
- w_fc1: bfloat16 [1664, 8192], P(None, 'tp'), may hold values from -0.15625 to 0.15625
- w_fc2: bfloat16 [8192, 1664], P('tp'), may hold values from -0.125 to 0.125
- merge_gain: float32 [1664], replicated, may hold values from 0.1 to 1.9
- w_merge: bfloat16 [6656, 1664], P('tp'), may hold values from -0.078125 to 0.078125
- slots: int32 [16, 256], P('req'), may hold values from 0 to 3071, as said below
- text: bfloat16 [16, 3072, 1664], P('req', 'tp'), may hold values from -6 to 6
- docs: int32 [16, 3072], P('req'), may hold values from 0 to 7, never falling along the last dimension, each value on 1 to 768 neighbouring positions
- dec_gain: float32 [1664], replicated, may hold values from 0.1 to 1.9
- w_qkv: bfloat16 [1664, 4992], P(None, 'tp'), may hold values from -0.2773501 to 0.2773501
- w_out: bfloat16 [1664, 1664], P('tp'), may hold values from -0.625 to 0.625
Outputs:
- decoded: bfloat16 [16, 3072, 1664], P('req', 'tp')
Inputs may be any that keep to these rules, and one draw needn't show every extreme that they name: `slots`: positions in a group are distinct; each image's 64 merged rows take consecutive positions in order, and image k lies within positions j * 768 to (j + 1) * 768 - 1 with j = (k + 2) mod 4; the image with j = 3 takes the last 64 positions of the prompt. `docs`: request numbers never fall along a prompt; each request spans 1 to 768 positions.
All inputs are finite; a program needn't handle non-finite values.
Results may differ from a plain program's by a relative error of at most 0.033.
Values may be sent and summed in bfloat16 or wider, within the bound.
A program may use at most 64 MiB of HBM per device.

v0:
```python
import math
import jax
import jax.numpy as jnp
from jax import lax
from jax.sharding import PartitionSpec as P

HD = 104
EPSILON = 1e-06


def layer_norm(values, gains):
    average = jnp.mean(values, axis=-1, keepdims=True)
    centred = values - average
    variance = jnp.mean(centred * centred, axis=-1, keepdims=True)
    return centred * lax.rsqrt(variance + EPSILON) * gains


def rms_norm(values, gains):
    return values * lax.rsqrt(jnp.mean(values * values, axis=-1, keepdims=True) + EPSILON) * gains


def attend(qkv_rows, doc_row, heads_here):
    seq_len = qkv_rows.shape[0]
    block_rows = min(512, seq_len)
    shaped = qkv_rows.reshape(seq_len, heads_here, 3, HD)
    queries = shaped[:, :, 0]
    key_rows = shaped[:, :, 1]
    value_rows = shaped[:, :, 2]
    key_pos = jnp.arange(seq_len)

    def one_block(block_index):
        offset = block_index * block_rows
        query_block = lax.dynamic_slice_in_dim(queries, offset, block_rows, 0)
        query_pos = offset + jnp.arange(block_rows)
        query_docs = lax.dynamic_slice_in_dim(doc_row, offset, block_rows, 0)
        scores = jnp.einsum(
            "qhe,khe->hqk", query_block, key_rows, preferred_element_type=jnp.float32
        ) / math.sqrt(HD)
        allowed = (key_pos[None, :] <= query_pos[:, None]) & (
            doc_row[None, :] == query_docs[:, None]
        )
        scores = jnp.where(allowed[None], scores, -1e30)
        largest = jnp.max(scores, axis=-1, keepdims=True)
        raised = jnp.where(allowed[None], jnp.exp(scores - largest), 0.0)
        weights = (raised / jnp.sum(raised, axis=-1, keepdims=True)).astype(jnp.bfloat16)
        blended = jnp.einsum(
            "hqk,khe->qhe", weights, value_rows, preferred_element_type=jnp.float32
        )
        return blended.astype(jnp.bfloat16).reshape(block_rows, heads_here * HD)

    blocks = lax.map(one_block, jnp.arange(seq_len // block_rows))
    return blocks.reshape(seq_len, heads_here * HD)


def shards(
    patches, vis_gain, w_fc1, w_fc2, merge_gain, w_merge, slots, text, docs, dec_gain, w_qkv, w_out
):
    patch_rows = patches[0]
    slot_row = slots[0]
    text_rows = text[0]
    doc_row = docs[0]
    width = patch_rows.shape[1]
    local_rows = patch_rows.shape[0]
    seq_here = text_rows.shape[0]
    wide_in = patch_rows.astype(jnp.float32)
    normed_in = layer_norm(wide_in, vis_gain).astype(jnp.bfloat16)
    hidden = jax.nn.gelu(
        jnp.dot(
            lax.all_gather(normed_in, "tp", axis=0, tiled=True),
            w_fc1,
            preferred_element_type=jnp.float32,
        ),
        approximate=False,
    ).astype(jnp.bfloat16)
    mlp_sum = lax.psum_scatter(
        jnp.dot(hidden, w_fc2, preferred_element_type=jnp.float32).astype(jnp.bfloat16),
        "tp",
        scatter_dimension=0,
        tiled=True,
    ).astype(jnp.float32)
    normed_out = layer_norm(wide_in + mlp_sum, merge_gain).astype(jnp.bfloat16)
    merge_in = normed_out.reshape(local_rows // 4, 4 * width)
    features = lax.all_to_all(merge_in, "tp", split_axis=1, concat_axis=0, tiled=True)
    merge_term = jnp.dot(features, w_merge, preferred_element_type=jnp.float32)
    merged_share = lax.psum_scatter(
        merge_term.astype(jnp.bfloat16), "tp", scatter_dimension=0, tiled=True
    )
    merged = lax.all_gather(merged_share, "tp", axis=0, tiled=True)
    positions = lax.axis_index("tp") * seq_here + jnp.arange(seq_here, dtype=jnp.int32)
    matches = slot_row[None, :] == positions[:, None]
    placed = jnp.dot(
        matches.astype(jnp.bfloat16), merged, preferred_element_type=jnp.float32
    ).astype(jnp.bfloat16)
    embedded = jnp.where(jnp.any(matches, axis=1)[:, None], placed, text_rows)
    dec_in = rms_norm(embedded.astype(jnp.float32), dec_gain).astype(jnp.bfloat16)
    qkv_rows = jnp.dot(
        lax.all_gather(dec_in, "tp", axis=0, tiled=True), w_qkv, preferred_element_type=jnp.float32
    ).astype(jnp.bfloat16)
    heads_here = qkv_rows.shape[1] // (3 * HD)
    attended = attend(qkv_rows, doc_row, heads_here)
    out_sum = lax.psum_scatter(
        jnp.dot(attended, w_out, preferred_element_type=jnp.float32).astype(jnp.bfloat16),
        "tp",
        scatter_dimension=0,
        tiled=True,
    ).astype(jnp.float32)
    decoded = (embedded.astype(jnp.float32) + out_sum).astype(jnp.bfloat16)
    return decoded[None]


def solution(mesh):
    placed = (
        P("req", "tp", None),
        P(),
        P(None, "tp"),
        P("tp", None),
        P(),
        P("tp", None),
        P("req", None),
        P("req", "tp", None),
        P("req", None),
        P(),
        P(None, "tp"),
        P("tp", None),
    )
    return jax.shard_map(
        shards, mesh=mesh, in_specs=placed, out_specs=P("req", "tp", None), check_vma=False
    )
```

profile of v0, /device:TPU:1, one launch (start us, length us, event | category | flops | bytes accessed | tf_op | source)
XLA Modules:
  0.0 623.6 jit_solution(15786397968516002857)
XLA Ops:
  6.5 1.2 convert_reduce_fusion
  7.7 1.2 fusion.66
  8.9 1.8 fusion.68
  10.7 0.0 all-gather.3.cloned.1.call-update
  10.7 0.0 reduce-scatter.4.cloned.1.call-start
  10.8 70.4 %all-gather.3.cloned.1.call-done = bf16[1024,1664]{1,0:T(8,128)(2,1)} async-done(((bf16[64,1664]{1,0:T(8,128)(2,1)}), bf16[1024,1664]{1,0:T(8,128)(2,1)}) %all-gather.3.cloned.1.call-update) | async-done | bytes 3407888 | tf_op jit(solution)/shard_map/all_gather | solution.py:69
  81.1 11.6 %convolution_convert_fusion.2 = bf16[1024,1664]{1,0:T(8,128)(2,1)} fusion(bf16[512,1664]{1,0:T(8,128)(2,1)S(1)} %copy-done, bf16[1024,1664]{1,0:T(8,128)(2,1)} %all-gather.3.cloned.1.call-done, bf16[1664,512]{1,0:T(8,128)(2,1)} %param.16), kind=kOutput, calls=%fused_computation.24 | convolution fusion | flops 3525443584 | bytes 10223616 | tf_op jit(solution)/shard_map/dot_general | solution.py:76
  92.7 0.0 reduce-scatter.6.cloned.1.call-start
  92.8 75.1 %reduce-scatter.4.cloned.1.call-done = bf16[64,1664]{1,0:T(8,128)(2,1)} async-done(((bf16[1024,1664]{1,0:T(8,128)(2,1)}), bf16[64,1664]{1,0:T(8,128)(2,1)}) %reduce-scatter.4.cloned.1.call-update) | async-done | bytes 213008 | tf_op jit(solution)/shard_map/reduce_scatter | solution.py:75
  167.9 1.1 fusion.70
  169.0 1.2 multiply_reduce_fusion.1
  170.2 1.1 multiply_convert_fusion.1
  171.3 0.3 all_to_all.14
  171.6 0.2 copy.18
  171.7 10.4 %all_to_all.19 = bf16[16,16,416]{2,0,1:T(8,128)(2,1)S(1)} all-to-all(bf16[16,16,416]{2,0,1:T(8,128)(2,1)S(1)} %copy.18), channel_id=1, replica_groups=mesh['req'=16,'tp'=16] {'tp'}, dimensions={1} | all-to-all | bytes 425984 | tf_op jit(solution)/shard_map/all_to_all | solution.py:83
  182.1 2.9 convolution_convert_fusion.3
  185.0 0.0 reduce-scatter.6.cloned.1.call-update
  185.0 0.0 all-gather.5.cloned.1.call-start
  185.1 0.2 compare_reduce_fusion
  185.3 68.8 %reduce-scatter.6.cloned.1.call-done = bf16[16,1664]{1,0:T(8,128)(2,1)} async-done(((bf16[256,1664]{1,0:T(8,128)(2,1)}), bf16[16,1664]{1,0:T(8,128)(2,1)}) %reduce-scatter.6.cloned.1.call-update) | async-done | bytes 53264 | tf_op jit(solution)/shard_map/reduce_scatter | solution.py:85
  254.1 30.6 %all_gather.10 = bf16[256,1664]{1,0:T(8,128)(2,1)S(1)} all-gather(bf16[16,1664]{1,0:T(8,128)(2,1)} %reduce-scatter.6.cloned.1.call-done), channel_id=1, replica_groups=mesh['req'=16,'tp'=16] {'tp'}, dimensions={0}, use_global_device_ids=true | all-gather | bytes 905216 | tf_op jit(solution)/shard_map/all_gather | solution.py:88
  284.7 1.6 multiply_reduce_fusion
  286.3 1.0 multiply_convert_fusion
  287.4 0.0 all-gather.5.cloned.1.call-update
  287.4 0.2 reduce-scatter.8.cloned.1.call-start
  287.6 132.2 %all-gather.5.cloned.1.call-done = bf16[3072,1664]{1,0:T(8,128)(2,1)} async-done(((bf16[192,1664]{1,0:T(8,128)(2,1)}), bf16[3072,1664]{1,0:T(8,128)(2,1)}) %all-gather.5.cloned.1.call-update) | async-done | bytes 10223632 | tf_op jit(solution)/shard_map/all_gather | solution.py:97
  419.8 7.8 %convolution_convert_fusion.1 = bf16[3072,312]{0,1:T(8,128)(2,1)S(1)} fusion(bf16[3072,1664]{1,0:T(8,128)(2,1)} %all-gather.5.cloned.1.call-done, bf16[1664,312]{0,1:T(8,128)(2,1)} %param.24), kind=kOutput, calls=%fused_computation.23 | convolution fusion | flops 3190726656 | bytes 13178880 | tf_op jit(solution)/shard_map/dot_general | solution.py:96
  427.6 1.3 slice_bitcast_fusion
  428.9 61.9 %while.11 = (s32[]{:T(128)}, bf16[6,512,104]{1,2,0:T(8,128)(2,1)}, s32[6]{0:T(128)S(1)}, s32[1,3072]{1,0:T(1,128)S(1)}, s32[3072]{0:T(1024)S(1)}, /*index=5*/bf1...) while((s32[]{:T(128)}, bf16[6,512,104]{1,2,0:T(8,128)(2,1)}, ...), condition=%wide.region_11.12_spmd.clone, body=%wide.region_8.11_spmd.clone.sunk | while | flops 690540032 | bytes 22987480 | solution.py:51
  428.9 0.5 dynamic_slice.23
  430.0 0.1 dynamic_slice.24
  430.1 3.2 fusion.121
  433.3 2.5 fusion.122
  435.8 3.4 fusion.123
  439.2 0.5 dynamic_slice.23
  440.4 0.1 dynamic_slice.24
  440.4 3.2 fusion.121
  443.6 2.5 fusion.122
  446.2 3.4 fusion.123
  449.6 0.5 dynamic_slice.23
  450.7 0.1 dynamic_slice.24
  450.8 3.2 fusion.121
  453.9 2.5 fusion.122
  456.5 3.4 fusion.123
  459.9 0.5 dynamic_slice.23
  461.0 0.1 dynamic_slice.24
  461.1 3.2 fusion.121
  464.3 2.5 fusion.122
  466.8 3.4 fusion.123
  470.2 0.5 dynamic_slice.23
  471.3 0.1 dynamic_slice.24
  471.4 3.2 fusion.121
  474.6 2.5 fusion.122
  477.1 3.4 fusion.123
  480.5 0.5 dynamic_slice.23
  481.6 0.1 dynamic_slice.24
  481.7 3.2 fusion.121
  484.9 2.5 fusion.122
  487.5 3.4 fusion.123
  490.9 1.1 copy.20
  492.0 5.4 convolution_convert_fusion
  497.5 0.0 reduce-scatter.8.cloned.1.call-update
  497.5 117.6 %reduce-scatter.8.cloned.1.call-done = bf16[192,1664]{1,0:T(8,128)(2,1)} async-done(((bf16[3072,1664]{1,0:T(8,128)(2,1)}), bf16[192,1664]{1,0:T(8,128)(2,1)}) %reduce-scatter.8.cloned.1.call-update) | async-done | bytes 638992 | tf_op jit(solution)/shard_map/reduce_scatter | solution.py:101
  615.0 2.0 fusion.61
  (42 shorter events, 0.1 us)
Async XLA Ops:
  6.5 74.6 %copy-start = (bf16[512,1664]{1,0:T(8,128)(2,1)S(1)}, bf16[512,1664]{1,0:T(8,128)(2,1)}, u32[]{:S(2)}) copy-start(bf16[512,1664]{1,0:T(8,128)(2,1)} %param.17) | copy-start | bytes 5111812
  6.5 74.6 %all-gather.3.cloned.1.call-start = ((), (), s32[]{:S(2)}) async-start(), calls=%async_computation.4 | async-start | bytes 3620864 | tf_op jit(solution)/shard_map/all_gather | solution.py:69
  10.7 157.2 %reduce-scatter.4.cloned.1.call-start = ((), (), s32[]{:S(2)}) async-start(), calls=%async_computation.5 | async-start | bytes 3620864 | tf_op jit(solution)/shard_map/reduce_scatter | solution.py:75
  92.7 75.2 %copy-start.1 = (bf16[1,64,1664]{2,1,0:T(8,128)(2,1)S(1)}, bf16[1,64,1664]{2,1,0:T(8,128)(2,1)}, u32[]{:S(2)}) copy-start(bf16[1,64,1664]{2,1,0:T(8,128)(2,1)} %param.14) | copy-start | bytes 638980
  92.7 77.5 %copy-start.5 = (f32[1664]{0:T(1024)S(1)}, f32[1664]{0:T(1024)}, u32[]{:S(2)}) copy-start(f32[1664]{0:T(1024)} %param.18) | copy-start | bytes 19972
  92.7 161.4 %reduce-scatter.6.cloned.1.call-start = ((), (), s32[]{:S(2)}) async-start(), calls=%async_computation.6 | async-start | bytes 905216 | tf_op jit(solution)/shard_map/reduce_scatter | solution.py:85
  171.6 13.5 %copy-start.7 = (s32[1,256]{1,0:T(1,128)S(1)}, s32[1,256]{1,0:T(1,128)}, u32[]{:S(2)}) copy-start(s32[1,256]{1,0:T(1,128)} %param.20) | copy-start | bytes 3076
  185.0 101.3 %copy-start.6 = (f32[1664]{0:T(1024)S(1)}, f32[1664]{0:T(1024)}, u32[]{:S(2)}) copy-start(f32[1664]{0:T(1024)} %param.23) | copy-start | bytes 19972
  185.0 234.8 %all-gather.5.cloned.1.call-start = ((), (), s32[]{:S(2)}) async-start(), calls=%async_computation.7 | async-start | bytes 10862592 | tf_op jit(solution)/shard_map/all_gather | solution.py:97
  287.4 327.7 %reduce-scatter.8.cloned.1.call-start = ((), (), s32[]{:S(2)}) async-start(), calls=%async_computation.8 | async-start | bytes 10862592 | tf_op jit(solution)/shard_map/reduce_scatter | solution.py:101
  427.6 1.3 copy-start.3
  428.9 63.1 %copy-start.4 = (bf16[104,1664]{1,0:T(8,128)(2,1)S(1)}, bf16[104,1664]{1,0:T(8,128)(2,1)}, u32[]{:S(2)}) copy-start(bf16[104,1664]{1,0:T(8,128)(2,1)} %param.25) | copy-start | bytes 1038340
  433.3 2.5 copy-start.2
  443.6 2.5 copy-start.2
  453.9 2.5 copy-start.2
  464.3 2.5 copy-start.2
  474.6 2.5 copy-start.2
  484.9 2.5 copy-start.2
Sparse Core Ops, SparseCore 0:
  10.8 70.2 all-gather.2
  92.9 75.0 reduce-scatter.3
  185.1 68.9 reduce-scatter.5
  287.5 132.2 all-gather.4
  497.6 117.3 reduce-scatter.7
where the time goes:
time: 624 us
  waiting for transfers between devices  464 us (74%)
  matrix products  68.8 us (11%)
  blocking collectives  41 us (7%)
  other arithmetic  25.9 us (4%)
  between operations  13.3 us (2%)
  local copies, waits for them, and re-layouts  6.75 us (1%)
    all_gather x1, waiting for transfers between devices, shards(): lax.all_gather(dec_in, 'tp', axis=0, tiled=True)  132 us
    reduce_scatter x1, waiting for transfers between devices, shards(): lax.psum_scatter(jnp.dot(attended, w_out, preferred_element_type=jnp.floa...  118 us
    reduce_scatter x1, waiting for transfers between devices, shards(): lax.psum_scatter(jnp.dot(hidden, w_fc2, preferred_element_type=jnp.float3...  75.1 us
    all_gather x1, waiting for transfers between devices, shards(): lax.all_gather(normed_in, 'tp', axis=0, tiled=True)  70.4 us
    reduce_scatter x1, waiting for transfers between devices, shards(): lax.psum_scatter(merge_term.astype(jnp.bfloat16), 'tp', scatter_dimension...  68.8 us
    all_gather x1, blocking collectives, shards(): merged = lax.all_gather(merged_share, 'tp', axis=0, tiled=True)  30.6 us
    dot_general x6, matrix products, one_block(): jnp.einsum('hqk,khe->qhe', weights, value_rows, preferred_element_type=jn...  20.5 us
    dot_general x6, matrix products, one_block(): jnp.einsum('qhe,khe->hqk', query_block, key_rows, preferred_element_type=...  19 us
  transfers between devices with their start and end apart: 5, of which 5 were waited for; matrix products, arithmetic and copies ran while one was open for 0% of the time, Pallas kernels for 0%

commit v1 on v0

--- a/solution.py
+++ b/solution.py
@@ -94,7 +94,11 @@
     embedded = jnp.where(jnp.any(matches, axis=1)[:, None], placed, text_rows)
     dec_in = rms_norm(embedded.astype(jnp.float32), dec_gain).astype(jnp.bfloat16)
     qkv_rows = jnp.dot(
-        lax.all_gather(dec_in, "tp", axis=0, tiled=True), w_qkv, preferred_element_type=jnp.float32
+        jnp.concatenate(
+            lax.all_to_all(jnp.stack([dec_in] * lax.axis_size("tp")), "tp", 0, 0), axis=0
+        ),
+        w_qkv,
+        preferred_element_type=jnp.float32,
     ).astype(jnp.bfloat16)
     heads_here = qkv_rows.shape[1] // (3 * HD)
     attended = attend(qkv_rows, doc_row, heads_here)

time: 624 us -> 726 us (1.16)
  waiting for transfers between devices: 464 us -> 556 us
    all_to_all x0 -> x1, waiting for transfers between devices: none -> 213 us  [shards(): lax.all_to_all(jnp.stack([dec_in] * lax.axis_size('tp')), 'tp', 0, 0)]
    all_gather x1 -> x0, waiting for transfers between devices: 132 us -> none  [shards(): lax.all_gather(dec_in, 'tp', axis=0, tiled=True)]
    reduce_scatter x1, waiting for transfers between devices: 118 us -> 129 us  [shards(): lax.psum_scatter(jnp.dot(attended, w_out, preferred_element_type=jnp.floa...]
where the time goes in v1:
time: 726 us; the launch traced here: 725 us
  waiting for transfers between devices  556 us (77%)
  matrix products  67.5 us (9%)
  blocking collectives  41 us (6%)
  other arithmetic  25 us (3%)
  local copies, waits for them, and re-layouts  13.3 us (2%)
  between operations  13.3 us (2%)
    all_to_all x1, waiting for transfers between devices, shards(): lax.all_to_all(jnp.stack([dec_in] * lax.axis_size('tp')), 'tp', 0, 0)  213 us
    reduce_scatter x1, waiting for transfers between devices, shards(): lax.psum_scatter(jnp.dot(attended, w_out, preferred_element_type=jnp.floa...  129 us
    reduce_scatter x1, waiting for transfers between devices, shards(): lax.psum_scatter(jnp.dot(hidden, w_fc2, preferred_element_type=jnp.float3...  75.1 us
    all_gather x1, waiting for transfers between devices, shards(): lax.all_gather(normed_in, 'tp', axis=0, tiled=True)  70.4 us
    reduce_scatter x1, waiting for transfers between devices, shards(): lax.psum_scatter(merge_term.astype(jnp.bfloat16), 'tp', scatter_dimension...  68.9 us
    all_gather x1, blocking collectives, shards(): merged = lax.all_gather(merged_share, 'tp', axis=0, tiled=True)  30.6 us
    dot_general x6, matrix products, one_block(): jnp.einsum('hqk,khe->qhe', weights, value_rows, preferred_element_type=jn...  20.5 us
    dot_general x6, matrix products, one_block(): jnp.einsum('qhe,khe->hqk', query_block, key_rows, preferred_element_type=...  19 us
  transfers between devices with their start and end apart: 5, of which 5 were waited for; matrix products, arithmetic and copies ran while one was open for 0% of the time, Pallas kernels for 0%

profile of v1, /device:TPU:1, one launch (start us, length us, event | category | flops | bytes accessed | tf_op | source)
XLA Modules:
  0.0 725.0 jit_solution(217852721181367010)
XLA Ops:
  6.5 1.2 convert_reduce_fusion
  7.7 1.2 fusion.66
  8.9 1.8 fusion.68
  10.7 0.0 all-gather.2.cloned.1.call-update
  10.7 0.0 reduce-scatter.4.cloned.1.call-start
  10.8 70.4 %all-gather.2.cloned.1.call-done = bf16[1024,1664]{1,0:T(8,128)(2,1)} async-done(((bf16[64,1664]{1,0:T(8,128)(2,1)}), bf16[1024,1664]{1,0:T(8,128)(2,1)}) %all-gather.2.cloned.1.call-update) | async-done | bytes 3407888 | tf_op jit(solution)/shard_map/all_gather | solution.py:69
  81.1 11.6 %convolution_convert_fusion.2 = bf16[1024,1664]{1,0:T(8,128)(2,1)} fusion(bf16[512,1664]{1,0:T(8,128)(2,1)S(1)} %copy-done, bf16[1024,1664]{1,0:T(8,128)(2,1)} %all-gather.2.cloned.1.call-done, bf16[1664,512]{1,0:T(8,128)(2,1)} %param.16), kind=kOutput, calls=%fused_computation.24 | convolution fusion | flops 3525443584 | bytes 10223616 | tf_op jit(solution)/shard_map/dot_general | solution.py:76
  92.7 0.0 reduce-scatter.4.cloned.1.call-update
  92.7 0.0 reduce-scatter.6.cloned.1.call-start
  92.8 75.1 %reduce-scatter.4.cloned.1.call-done = bf16[64,1664]{1,0:T(8,128)(2,1)} async-done(((bf16[1024,1664]{1,0:T(8,128)(2,1)}), bf16[64,1664]{1,0:T(8,128)(2,1)}) %reduce-scatter.4.cloned.1.call-update) | async-done | bytes 213008 | tf_op jit(solution)/shard_map/reduce_scatter | solution.py:75
  167.9 1.1 fusion.70
  169.0 1.2 multiply_reduce_fusion.1
  170.2 1.1 multiply_convert_fusion.1
  171.3 1.0 all_to_all.17
  172.3 1.1 copy.18
  173.4 10.4 %all_to_all.24 = bf16[16,16,416]{2,0,1:T(8,128)(2,1)S(1)} all-to-all(bf16[16,16,416]{2,0,1:T(8,128)(2,1)S(1)} %copy.18), channel_id=1, replica_groups=mesh['req'=16,'tp'=16] {'tp'}, dimensions={1} | all-to-all | bytes 425984 | tf_op jit(solution)/shard_map/all_to_all | solution.py:83
  183.8 1.5 convolution_convert_fusion.3
  185.4 0.2 compare_reduce_fusion
  185.6 68.9 %reduce-scatter.6.cloned.1.call-done = bf16[16,1664]{1,0:T(8,128)(2,1)} async-done(((bf16[256,1664]{1,0:T(8,128)(2,1)}), bf16[16,1664]{1,0:T(8,128)(2,1)}) %reduce-scatter.6.cloned.1.call-update) | async-done | bytes 53264 | tf_op jit(solution)/shard_map/reduce_scatter | solution.py:85
  254.4 30.6 %all_gather.7 = bf16[256,1664]{1,0:T(8,128)(2,1)S(1)} all-gather(bf16[16,1664]{1,0:T(8,128)(2,1)} %reduce-scatter.6.cloned.1.call-done), channel_id=1, replica_groups=mesh['req'=16,'tp'=16] {'tp'}, dimensions={0}, use_global_device_ids=true | all-gather | bytes 905216 | tf_op jit(solution)/shard_map/all_gather | solution.py:88
  285.0 1.6 multiply_reduce_fusion
  286.6 0.2 multiply_convert_fusion
  286.8 4.9 stack.2
  291.7 4.8 all-to-all-start.1
  296.5 0.2 reduce-scatter.8.cloned.1.call-start
  296.8 213.4 %all-to-all-done.1 = bf16[16,192,1664]{2,1,0:T(8,128)(2,1)} async-done(((bf16[16,192,1664]{2,1,0:T(8,128)(2,1)}), bf16[16,192,1664]{2,1,0:T(8,128)(2,1)}, u32[]{:S(2)}, u32[]{:S(2)}) %all-to-all-start.1) | async-done | bytes 10223648 | tf_op jit(solution)/shard_map/all_to_all | solution.py:98
  510.2 7.8 %convolution_convert_fusion.1 = bf16[3072,312]{0,1:T(8,128)(2,1)S(1)} fusion(bf16[3072,1664]{1,0:T(8,128)(2,1)} %bitcast.6, bf16[1664,312]{0,1:T(8,128)(2,1)} %param.24), kind=kOutput, calls=%fused_computation.23 | convolution fusion | flops 3190726656 | bytes 13178880 | tf_op jit(solution)/shard_map/dot_general | solution.py:96
  518.0 1.3 slice_bitcast_fusion
  519.3 61.9 %while.11 = (s32[]{:T(128)}, bf16[6,512,104]{1,2,0:T(8,128)(2,1)}, s32[6]{0:T(128)S(1)}, s32[1,3072]{1,0:T(1,128)S(1)}, s32[3072]{0:T(1024)S(1)}, /*index=5*/bf1...) while((s32[]{:T(128)}, bf16[6,512,104]{1,2,0:T(8,128)(2,1)}, ...), condition=%wide.region_11.12_spmd.clone, body=%wide.region_8.11_spmd.clone.sunk | while | flops 690540032 | bytes 22987480 | solution.py:51
  519.3 0.5 dynamic_slice.23
  520.4 0.1 dynamic_slice.24
  520.5 3.2 fusion.121
  523.7 2.5 fusion.122
  526.2 3.4 fusion.123
  529.7 0.5 dynamic_slice.23
  530.8 0.1 dynamic_slice.24
  530.8 3.2 fusion.121
  534.0 2.5 fusion.122
  536.6 3.4 fusion.123
  540.0 0.5 dynamic_slice.23
  541.1 0.1 dynamic_slice.24
  541.2 3.2 fusion.121
  544.4 2.5 fusion.122
  546.9 3.4 fusion.123
  550.3 0.5 dynamic_slice.23
  551.4 0.1 dynamic_slice.24
  551.5 3.2 fusion.121
  554.7 2.5 fusion.122
  557.2 3.4 fusion.123
  560.6 0.5 dynamic_slice.23
  561.7 0.1 dynamic_slice.24
  561.8 3.2 fusion.121
  565.0 2.5 fusion.122
  567.5 3.4 fusion.123
  571.0 0.5 dynamic_slice.23
  572.1 0.1 dynamic_slice.24
  572.1 3.2 fusion.121
  575.3 2.5 fusion.122
  577.9 3.4 fusion.123
  581.3 1.1 copy.20
  582.4 5.4 convolution_convert_fusion
  587.9 0.0 reduce-scatter.8.cloned.1.call-update
  587.9 128.5 %reduce-scatter.8.cloned.1.call-done = bf16[192,1664]{1,0:T(8,128)(2,1)} async-done(((bf16[3072,1664]{1,0:T(8,128)(2,1)}), bf16[192,1664]{1,0:T(8,128)(2,1)}) %reduce-scatter.8.cloned.1.call-update) | async-done | bytes 638992 | tf_op jit(solution)/shard_map/reduce_scatter | solution.py:105
  716.4 2.0 fusion.61
  (44 shorter events, 0.1 us)
Async XLA Ops:
  6.5 74.6 %copy-start = (bf16[512,1664]{1,0:T(8,128)(2,1)S(1)}, bf16[512,1664]{1,0:T(8,128)(2,1)}, u32[]{:S(2)}) copy-start(bf16[512,1664]{1,0:T(8,128)(2,1)} %param.17) | copy-start | bytes 5111812
  6.5 74.6 %all-gather.2.cloned.1.call-start = ((), (), s32[]{:S(2)}) async-start(), calls=%async_computation.5 | async-start | bytes 3620864 | tf_op jit(solution)/shard_map/all_gather | solution.py:69
  10.7 157.2 %reduce-scatter.4.cloned.1.call-start = ((), (), s32[]{:S(2)}) async-start(), calls=%async_computation.6 | async-start | bytes 3620864 | tf_op jit(solution)/shard_map/reduce_scatter | solution.py:75
  92.7 75.2 %copy-start.1 = (bf16[1,64,1664]{2,1,0:T(8,128)(2,1)S(1)}, bf16[1,64,1664]{2,1,0:T(8,128)(2,1)}, u32[]{:S(2)}) copy-start(bf16[1,64,1664]{2,1,0:T(8,128)(2,1)} %param.14) | copy-start | bytes 638980
  92.7 77.5 %copy-start.6 = (f32[1664]{0:T(1024)S(1)}, f32[1664]{0:T(1024)}, u32[]{:S(2)}) copy-start(f32[1664]{0:T(1024)} %param.18) | copy-start | bytes 19972
  92.7 91.0 %copy-start.2 = (bf16[416,1664]{1,0:T(8,128)(2,1)S(1)}, bf16[416,1664]{1,0:T(8,128)(2,1)}, u32[]{:S(2)}) copy-start(bf16[416,1664]{1,0:T(8,128)(2,1)} %param.19) | copy-start | bytes 4153348
  92.7 161.7 %reduce-scatter.6.cloned.1.call-start = ((), (), s32[]{:S(2)}) async-start(), calls=%async_computation.7 | async-start | bytes 905216 | tf_op jit(solution)/shard_map/reduce_scatter | solution.py:85
  172.3 13.1 %copy-start.8 = (s32[1,256]{1,0:T(1,128)S(1)}, s32[1,256]{1,0:T(1,128)}, u32[]{:S(2)}) copy-start(s32[1,256]{1,0:T(1,128)} %param.20) | copy-start | bytes 3076
  185.3 101.3 %copy-start.7 = (f32[1664]{0:T(1024)S(1)}, f32[1664]{0:T(1024)}, u32[]{:S(2)}) copy-start(f32[1664]{0:T(1024)} %param.23) | copy-start | bytes 19972
  291.7 218.5 %all-to-all-start.1 = ((bf16[16,192,1664]{2,1,0:T(8,128)(2,1)}), bf16[16,192,1664]{2,1,0:T(8,128)(2,1)}, u32[]{:S(2)}, u32[]{:S(2)}) async-start(bf16[16,192,1664]{2,1,0:T(8,128)(2,1)} %stack.2), calls=%async_computation.3 | async-start | bytes 20447232 | tf_op jit(solution)/shard_map/all_to_all | solution.py:98
  296.5 419.9 %reduce-scatter.8.cloned.1.call-start = ((), (), s32[]{:S(2)}) async-start(), calls=%async_computation.8 | async-start | bytes 10862592 | tf_op jit(solution)/shard_map/reduce_scatter | solution.py:105
  518.0 1.3 copy-start.4
  519.3 63.1 %copy-start.5 = (bf16[104,1664]{1,0:T(8,128)(2,1)S(1)}, bf16[104,1664]{1,0:T(8,128)(2,1)}, u32[]{:S(2)}) copy-start(bf16[104,1664]{1,0:T(8,128)(2,1)} %param.25) | copy-start | bytes 1038340
  523.7 2.5 copy-start.3
  534.0 2.5 copy-start.3
  544.3 2.5 copy-start.3
  554.7 2.5 copy-start.3
  565.0 2.5 copy-start.3
  575.3 2.5 copy-start.3
Sparse Core Ops, SparseCore 0:
  10.8 70.2 all-gather.1
  92.9 75.0 reduce-scatter.3
  185.5 68.9 reduce-scatter.5
  588.0 128.3 reduce-scatter.7
